TPU v7x, 32 devices: a whole 2x2x4 slice. The times are simulated.
32 devices in a mesh: tm: 2 (over core), height: 8 (over z, y), head: 2 (over x).
Axes of the slice: x: 2, y: 2, z: 4, core: 2. Of those that a mesh axis runs over, the one named last changes fastest.
Arguments:
- queries: bfloat16 [4, 16, 64, 1280], P('tm', 'height', None, 'head'), may hold values from -22 to 22
- keys_values: bfloat16 [2, 4, 16, 64, 1280], P(None, 'tm', 'height', None, 'head'), may hold values from -7 to 7
- out_weight: bfloat16 [1280, 5120], P('head'), may hold values from -0.15625 to 0.15625
Outputs:
- mixed: bfloat16 [64, 4, 16, 5120], P('head', 'tm', 'height')
All inputs are finite; a program needn't handle non-finite values.
Results may differ from a plain program's by a relative error of at most 0.013.
Values may be sent and summed in bfloat16 or wider, within the bound.
A program may use at most 128 MiB of HBM per device.

v0:
```python
import math

import jax
import jax.numpy as jnp
from jax import lax
from jax.sharding import PartitionSpec as P

HD = 128
TILE = 16
WINDOW = 3
PAD_ROWS = 2
VALID_COLS = 52


masked_value = -1e30


def from_partner(value, axis, apart):
    mask = 2**apart
    pairs = [(source, source ^ mask) for source in range(lax.axis_size(axis))]
    return lax.ppermute(value, axis, pairs)


def window_start(tile_index, tile_count):
    span_size = min(tile_count, WINDOW)
    return (jnp.clip(tile_index - 1, 0, tile_count - span_size), span_size)


def column_groups(col_tiles):
    col_span = min(col_tiles, WINDOW)
    grouped = []
    for col_tile in range(col_tiles):
        key_begin = max(0, min(col_tile - 1, col_tiles - col_span))
        if len(grouped) > 0 and grouped[-1][2] == key_begin:
            grouped[-1] = (grouped[-1][0], col_tile + 1, key_begin)
        else:
            grouped.append((col_tile, col_tile + 1, key_begin))
    return (grouped, col_span)


def edge_frame(local_keys, side_index):
    last_frame = local_keys.shape[1] - 1
    begin = (1 - side_index) * last_frame
    return lax.dynamic_slice_in_dim(local_keys, begin, 1, 1)


def attach_rim(local_keys, rim_frame, side_index):
    joined = jnp.concatenate([rim_frame, local_keys, rim_frame], axis=1)
    begin = 1 - side_index
    return lax.dynamic_slice_in_dim(joined, begin, local_keys.shape[1] + 1, 1)


def on_device(queries, keys_values, out_weight):
    frames_dev, rows_dev, col_count, width_dev = queries.shape
    heads_dev = width_dev // HD
    frame_count = frames_dev * lax.axis_size("tm")
    frame_rows = rows_dev * lax.axis_size("height")
    valid_rows = frame_rows - PAD_ROWS
    row_tiles = frame_rows // TILE
    side_index = lax.axis_index("tm")
    first_frame = side_index * frames_dev
    first_row = lax.axis_index("height") * rows_dev
    score_scale = 1.0 / math.sqrt(HD)
    query_frames = first_frame + jnp.arange(frames_dev, dtype=jnp.int32)
    frame_low, frame_span = window_start(query_frames, frame_count)
    query_rows = first_row + jnp.arange(rows_dev, dtype=jnp.int32)
    row_tile_low, row_span = window_start(query_rows // TILE, row_tiles)
    row_low = row_tile_low * TILE
    row_high = row_low + row_span * TILE
    grouped, col_span = column_groups(col_count // TILE)
    key_width = col_span * TILE
    query_groups = []
    col_fits = []
    starters = []
    for first_tile, last_tile, key_tile in grouped:
        selected = queries[:, :, first_tile * TILE : last_tile * TILE, :]
        query_groups.append(selected.reshape(-1, width_dev))
        col_fits.append(key_tile * TILE + jnp.arange(key_width, dtype=jnp.int32) < VALID_COLS)
        query_total = selected.shape[0] * selected.shape[1] * selected.shape[2]
        starters.append(
            tuple(
                (
                    (
                        jnp.full((query_total,), masked_value, jnp.float32),
                        jnp.zeros((query_total,), jnp.float32),
                        jnp.zeros((query_total, HD), jnp.float32),
                    )
                    for member in range(heads_dev)
                )
            )
        )
    initial = tuple(starters)
    whole_rows = lax.all_gather(keys_values, "height", axis=2, tiled=True)
    rim_frame = from_partner(edge_frame(whole_rows, side_index), "tm", 0)
    with_rims = attach_rim(whole_rows, rim_frame, side_index)
    extended = with_rims.shape[1]
    row_piece = with_rims.shape[2]
    key_frames = first_frame - side_index + jnp.arange(extended, dtype=jnp.int32)
    key_rows = jnp.arange(row_piece, dtype=jnp.int32)
    time_fits = (key_frames[None, :] >= frame_low[:, None]) & (
        key_frames[None, :] < frame_low[:, None] + frame_span
    )
    row_fits = (key_rows[None, :] >= row_low[:, None]) & (key_rows[None, :] < row_high[:, None])
    row_fits = row_fits & (key_rows[None, :] < valid_rows)
    updated = []
    for add_group_id, (add_first_tile, add_last_tile, add_key_tile) in enumerate(grouped):
        add_query_cols = (add_last_tile - add_first_tile) * TILE
        visible = (
            time_fits[:, None, None, :, None, None]
            & row_fits[None, :, None, None, :, None]
            & col_fits[add_group_id][None, None, None, None, None, :]
        )
        visible = jnp.broadcast_to(
            visible, (frames_dev, rows_dev, add_query_cols, extended, row_piece, key_width)
        )
        visible = visible.reshape(
            frames_dev * rows_dev * add_query_cols, extended * row_piece * key_width
        )
        col_begin = add_key_tile * TILE
        key_block = with_rims[0, :, :, col_begin : col_begin + key_width, :].reshape(-1, width_dev)
        value_block = with_rims[1, :, :, col_begin : col_begin + key_width, :].reshape(
            -1, width_dev
        )
        head_states = []
        for member in range(heads_dev):
            running_max, running_sum, running_out = initial[add_group_id][member]
            head_query = query_groups[add_group_id][:, member * HD : (member + 1) * HD]
            head_keys = key_block[:, member * HD : (member + 1) * HD]
            head_values = value_block[:, member * HD : (member + 1) * HD]
            scores = (
                jnp.einsum("qd,kd->qk", head_query, head_keys, preferred_element_type=jnp.float32)
                * score_scale
            )
            scores = jnp.where(visible, scores, masked_value)
            new_max = jnp.maximum(running_max, jnp.max(scores, axis=1))
            weights = jnp.where(visible, jnp.exp(scores - new_max[:, None]), 0.0)
            new_sum = jnp.sum(weights, axis=1)
            new_out = jnp.dot(
                weights.astype(jnp.bfloat16), head_values, preferred_element_type=jnp.float32
            )
            head_states.append((new_max, new_sum, new_out))
        updated.append(tuple(head_states))
    final_state = tuple(updated)
    pieces = []
    for group_id, (first_tile, last_tile, key_tile) in enumerate(grouped):
        query_cols = (last_tile - first_tile) * TILE
        head_parts = [state[2] / state[1][:, None] for state in final_state[group_id]]
        group_out = jnp.concatenate(head_parts, axis=1).astype(jnp.bfloat16)
        group_out = group_out.reshape(frames_dev, rows_dev, query_cols, width_dev)
        pieces.append(jnp.transpose(group_out, (2, 0, 1, 3)))
    attended = jnp.concatenate(pieces, axis=0)
    return lax.psum_scatter(
        jnp.einsum(
            "cfrh,hd->cfrd", attended, out_weight, preferred_element_type=jnp.float32
        ).astype(jnp.bfloat16),
        "head",
        scatter_dimension=0,
        tiled=True,
    )


def solution(mesh):
    placed = (
        P("tm", "height", None, "head"),
        P(None, "tm", "height", None, "head"),
        P("head", None),
    )
    return jax.shard_map(
        on_device,
        mesh=mesh,
        in_specs=placed,
        out_specs=P("head", "tm", "height", None),
        check_vma=False,
    )
```

profile of v0, /device:TPU:28, one launch (start us, length us, event | category | flops | bytes accessed | tf_op | source)
XLA Modules:
  0.0 176.2 jit_solution(4382157549609009276)
XLA Ops:
  6.5 0.7 all-gather.2.cloned.1.call-update
  7.3 0.0 reduce-scatter.2.cloned.1.call-start
  7.3 86.7 %all-gather.2.cloned.1.call-done = bf16[2,2,16,64,640]{4,3,2,1,0:T(8,128)(2,1)} async-done(((bf16[2,2,2,64,640]{4,3,2,1,0:T(8,128)(2,1)}), bf16[2,2,16,64,640]{4,3,2,1,0:T(8,128)(2,1)}) %all-gather.2.cloned.1.call-update) | async-done | bytes 5242896 | tf_op jit(solution)/shard_map/all_gather | solution.py:93
  94.0 3.5 %constant_dynamic-slice_fusion = bf16[2,1,16,64,640]{4,3,2,1,0:T(8,128)(2,1)} fusion(bf16[2,2,16,64,640]{4,3,2,1,0:T(8,128)(2,1)} %all-gather.2.cloned.1.call-done, s32[]{:T(128)S(6)} %select_n.80), kind=kLoop, calls=%fused_computation.160 | loop fusion | bytes 5242884 | tf_op jit(solution)/shard_map/dynamic_slice | solution.py:44
  97.5 0.0 collective-permute-start
  97.6 0.1 compare_and_fusion
  97.7 0.1 and_and_fusion
  97.7 0.1 broadcast_and_fusion.2
  97.8 0.1 broadcast_and_fusion.1
  97.9 0.2 broadcast_in_dim.29
  98.1 1.5 reshape.255
  99.7 0.4 copy.6
  100.1 0.0 copy-start
  100.1 0.2 broadcast_in_dim.32
  100.3 1.5 reshape.257
  101.8 0.4 copy.16
  102.2 0.5 collective-permute-done
  102.8 5.7 %fusion.1 = bf16[2,3,16,64,640]{4,3,2,1,0:T(8,128)(2,1)S(1)} fusion(s32[]{:T(128)S(6)} %select_n.81, bf16[2,1,16,64,640]{4,3,2,1,0:T(8,128)(2,1)} %collective-permute-done, bf16[2,2,16,64,640]{4,3,2,1,0:T(8,128)(2,1)} %all-gather.2.cloned.1.call-done), kind=kLoop, calls=%fused_computation.4 | loop fusion | flops 7864320 | bytes 15728644 | tf_op jit(solution)/shard_map/concatenate | solution.py:48
  108.5 1.7 fusion.131
  110.2 0.5 fusion.139
  110.7 0.5 fusion.140
  111.2 0.5 fusion.141
  111.7 0.5 fusion.142
  112.2 0.5 fusion.138
  112.7 0.5 fusion.134
  113.2 0.5 fusion.135
  113.6 0.5 fusion.136
  114.1 0.5 fusion.137
  114.6 0.5 fusion.133
  115.2 1.1 fusion.45
  116.2 0.5 fusion.31
  116.7 0.5 fusion.30
  117.2 0.5 fusion.29
  117.6 0.5 fusion.28
  118.1 0.5 fusion.27
  118.7 1.1 fusion.55
  119.7 0.0 slice-start
  119.7 0.5 fusion.36
  120.2 0.5 fusion.35
  120.7 0.0 slice-start.1
  120.7 0.5 fusion.34
  121.2 0.5 fusion.33
  121.7 0.5 fusion.32
  122.3 0.6 slice-done.1
  122.9 3.8 %fusion.4 = bf16[64,2,2,5120]{3,0,2,1:T(8,128)(2,1)} fusion(bf16[640,5120]{1,0:T(8,128)(2,1)S(1)} %bitcast.112, bf16[32,2,2,640]{3,0,2,1:T(8,128)(2,1)S(1)} %bitcast.110, bf16[32,2,2,640]{3,0,2,1:T(8,128)(2,1)S(1)} %bitcast.109), kind=kOutput, calls=%fused_computation.7 | convolution fusion | flops 1679687680 | bytes 9502720 | tf_op jit(solution)/shard_map/cfrh,hd->cfrd/dot_general | solution.py:153
  126.7 0.0 reduce-scatter.2.cloned.1.call-update
  126.7 38.9 %reduce-scatter.2.cloned.1.call-done = bf16[32,2,2,5120]{3,0,2,1:T(8,128)(2,1)} async-done(((bf16[64,2,2,5120]{3,0,2,1:T(8,128)(2,1)}), bf16[32,2,2,5120]{3,0,2,1:T(8,128)(2,1)}) %reduce-scatter.2.cloned.1.call-update) | async-done | bytes 1310736 | tf_op jit(solution)/shard_map/reduce_scatter | solution.py:152
  165.6 3.7 %copy.25 = bf16[32,2,2,5120]{3,2,1,0:T(2,128)(2,1)} copy(bf16[32,2,2,5120]{3,0,2,1:T(8,128)(2,1)} %reduce-scatter.2.cloned.1.call-done) | data formatting | bytes 2621440 | tf_op jit(solution)/shard_map/reduce_scatter | solution.py:152
  (30 shorter events, 0.2 us)
Async XLA Ops:
  6.5 87.5 %all-gather.2.cloned.1.call-start = ((), (), s32[]{:S(2)}) async-start(), calls=%async_computation.1 | async-start | bytes 5898240 | tf_op jit(solution)/shard_map/all_gather | solution.py:93
  7.3 158.3 %reduce-scatter.2.cloned.1.call-start = ((), (), s32[]{:S(2)}) async-start(), calls=%async_computation.2 | async-start | bytes 3932160 | tf_op jit(solution)/shard_map/reduce_scatter | solution.py:152
  97.5 5.3 %collective-permute-start = (bf16[2,1,16,64,640]{4,3,2,1,0:T(8,128)(2,1)}, bf16[2,1,16,64,640]{4,3,2,1,0:T(8,128)(2,1)}, u32[]{:S(2)}, u32[]{:S(2)}) collective-permute-start(bf16[2,1,16,64,640]{4,3,2,1,0:T(8,128)(2,1)} %constant_dynamic-slice_fusion), channel_id=1, source_target_pairs={{0,16},{16,0},{1,17},{17,1},{2,18},{18,2},{3,19},{19,3},{4,20},{20... | collective-permute-start | bytes 7864328 | tf_op jit(solution)/shard_map/ppermute | solution.py:21
  100.1 2.1 %copy-start = (bf16[2,2,64,640]{3,2,1,0:T(8,128)(2,1)S(1)}, bf16[2,2,64,640]{3,2,1,0:T(8,128)(2,1)}, u32[]{:S(2)}) copy-start(bf16[2,2,64,640]{3,2,1,0:T(8,128)(2,1)} %param.3) | copy-start | bytes 983044
  119.7 2.6 %slice-start = ((s8[6553600]{0:T(1024)(128)(4,1)}), s8[4194304]{0:T(1024)(128)(4,1)S(1)}, s32[]{:S(2)}) async-start(s8[6553600]{0:T(1024)(128)(4,1)} %bitcast.111), calls=%async_computation.3 | async-start | bytes 8388608
  120.7 2.2 %slice-start.1 = ((s8[6553600]{0:T(1024)(128)(4,1)}), s8[2359296]{0:T(1024)(128)(4,1)S(1)}, s32[]{:S(2)}) async-start(s8[6553600]{0:T(1024)(128)(4,1)} %bitcast.111), calls=%async_computation.4 | async-start | bytes 4718592
Sparse Core Ops, SparseCore 0:
  9.5 84.3 all-gather.1
  126.8 38.7 reduce-scatter.1
where the time goes:
time: 178 us; the launch traced here: 176 us
  waiting for transfers between devices  127 us (71%)
  local copies, waits for them, and re-layouts  13.9 us (8%)
  between operations  13.7 us (8%)
  matrix products  13.4 us (8%)
  other arithmetic  8.24 us (5%)
    all_gather x1, waiting for transfers between devices, on_device(): whole_rows = lax.all_gather(keys_values, 'height', axis=2, tiled=True)  86.7 us
    reduce_scatter x1, waiting for transfers between devices, on_device(): lax.psum_scatter(jnp.einsum('cfrh,hd->cfrd', attended, out_weight, prefer...  38.9 us
    concatenate x1, other arithmetic, attach_rim(): joined = jnp.concatenate([rim_frame, local_keys, rim_frame], axis=1)  5.71 us
    dot_general x10, matrix products, on_device(): jnp.einsum('qd,kd->qk', head_query, head_keys, preferred_element_type=jnp...  4.89 us
    dot_general x10, matrix products, on_device(): jnp.dot(weights.astype(jnp.bfloat16), head_values, preferred_element_type...  4.72 us
    reshape x4, local copies, waits for them, and re-layouts, on_device(): visible.reshape(frames_dev * rows_dev * add_query_cols, extended * row_pi...  3.79 us
    dot_general x1, matrix products, on_device(): jnp.einsum('cfrh,hd->cfrd', attended, out_weight, preferred_element_type=...  3.77 us
    reduce_scatter x1, local copies, waits for them, and re-layouts, on_device(): lax.psum_scatter(jnp.einsum('cfrh,hd->cfrd', attended, out_weight, prefer...  3.72 us
  transfers between devices with their start and end apart: 3, of which 3 were waited for; matrix products, arithmetic and copies ran while one was open for 3% of the time, Pallas kernels for 0%

commit v1 on v0

v1 whole, which is shorter than its diff:
```python
import functools
import math

import jax
import jax.numpy as jnp
from jax import lax
from jax.experimental import pallas as pl
from jax.experimental.pallas import tpu as pltpu
from jax.sharding import PartitionSpec as P

HD = 128
TILE = 16
WINDOW = 3
PAD_ROWS = 2
VALID_COLS = 52
MESH = pl.DeviceIdType.MESH
UP, DOWN, ACROSS, CORE = 0, 1, 2, 3
PIECE = 512

masked_value = -1e30


def kernel(
    n_height,
    n_head,
    rows_dev,
    q_ref,
    kv_hbm,
    w_hbm,
    out_ref,
    kv,
    w,
    bias,
    top,
    total,
    acc,
    att,
    outbox,
    inbox,
    own_sem,
    w_sem,
    send_sem,
    recv_sem,
    part_send,
    part_recv,
):
    lines = n_height // 2
    tokens, width = q_ref.shape
    heads = width // HD
    key_count = rows_dev * VALID_COLS
    model = w.shape[1]
    pieces = model // PIECE
    share = tokens // n_head
    last = lines - 1

    side = lax.axis_index("tm")
    place = lax.axis_index("height")
    group = lax.axis_index("head")
    z = place // 2
    y = place % 2
    has_own = place < n_height - 1

    weight_copy = pltpu.make_async_copy(w_hbm, w, w_sem)
    weight_copy.start()
    own_copy = pltpu.make_async_copy(kv_hbm, kv.at[place, 0:2], own_sem)
    own_copy.start()

    barrier = pltpu.get_barrier_semaphore()

    def greet(target):
        pl.semaphore_signal(barrier, inc=1, device_id=target, device_id_type=MESH)

    @pl.when(z < last)
    def _():
        greet({"height": place + 2})

    @pl.when(z > 0)
    def _():
        greet({"height": place - 2})

    greet({"height": place + 1 - 2 * y})
    greet({"tm": 1 - side})
    for step in range(1, n_head):
        greet({"head": lax.rem(group + step, n_head)})

    def link(direction, slot, frame):
        target = {
            UP: {"height": jnp.minimum(place + 2, n_height - 1)},
            DOWN: {"height": jnp.maximum(place - 2, 0)},
            ACROSS: {"height": place + 1 - 2 * y},
            CORE: {"tm": 1 - side},
        }[direction]
        landing = 2 if direction == CORE else frame
        return pltpu.make_async_remote_copy(
            src_ref=kv.at[slot, frame],
            dst_ref=kv.at[slot, landing],
            send_sem=send_sem.at[direction, slot, frame],
            recv_sem=recv_sem.at[slot, landing],
            device_id=target,
            device_id_type=MESH,
        )

    def on_line(d, sign):
        zs = z + sign * d
        real = (zs >= 0) & (zs < lines) & ((d > 0) | has_own)
        if sign > 0:
            real = real & (d > 0)
        proxied = (zs == last) & (y == 1)
        slot = jnp.clip(jnp.where(proxied, 2 * last, 2 * zs + y), 0, n_height - 1)
        up = real & (z < last) & ((sign < 0) | (d == 0))
        down = real & (z > 0) & ((sign > 0) | (d == 0))
        across = real & ((zs != last) | ((z == last) & (y == 0)))
        return real, slot, up, down, across

    def off_line(d, sign):
        zs = z + sign * d
        proxy = (z == last) & (y == 1) & (zs == last)
        real = (d >= 0) & (zs >= 0) & (zs < lines) & ((zs != last) | proxy)
        if sign > 0:
            real = real & (d > 0)
        slot = jnp.clip(2 * zs + 1 - y, 0, n_height - 1)
        return real, slot, proxy & real

    def line_sends(d, sign, act):
        real, slot, up, down, across = on_line(d, sign)
        for frame in (0, 1):
            if act == "start":

                @pl.when(real & (d > 0))
                def _():
                    link(UP, slot, frame).wait_recv()

            for flag, direction in ((up, UP), (down, DOWN), (across, ACROSS)):

                @pl.when(flag)
                def _():
                    copy = link(direction, slot, frame)
                    copy.start() if act == "start" else copy.wait_send()

            if frame == 0:

                @pl.when(real)
                def _():
                    copy = link(CORE, slot, 0)
                    copy.start() if act == "start" else copy.wait_send()

    def cross_sends(d, sign, act):
        real, slot, proxy = off_line(d, sign)
        for frame in (0, 1):
            if act == "start":

                @pl.when(real)
                def _():
                    link(ACROSS, slot, frame).wait_recv()

            @pl.when(proxy)
            def _():
                copy = link(DOWN, slot, frame)
                copy.start() if act == "start" else copy.wait_send()

            if frame == 0:

                @pl.when(real)
                def _():
                    copy = link(CORE, slot, 0)
                    copy.start() if act == "start" else copy.wait_send()

    factor = math.log2(math.e) / math.sqrt(HD)

    def attend(slot):
        pltpu.make_async_remote_copy(
            src_ref=kv.at[slot, 2],
            dst_ref=kv.at[slot, 2],
            send_sem=send_sem.at[CORE, slot, 0],
            recv_sem=recv_sem.at[slot, 2],
            device_id={"tm": 1 - side},
            device_id_type=MESH,
        ).wait_recv()
        for head in range(heads):
            lanes = slice(head * HD, (head + 1) * HD)
            query = q_ref[:, lanes]
            scores = []
            for frame in range(3):
                key = kv[slot, frame, 0:key_count, lanes]
                score = lax.dot_general(
                    query, key, (((1,), (1,)), ((), ())), preferred_element_type=jnp.float32
                )
                scores.append(score * factor + bias[...])
            largest = jnp.maximum(jnp.maximum(scores[0], scores[1]), scores[2])
            old_top = top[head]
            new_top = jnp.maximum(old_top, jnp.max(largest, axis=1, keepdims=True))
            alpha = jnp.exp2(old_top - new_top)
            top[head] = new_top
            added = None
            mixed = None
            for frame in range(3):
                weight = jnp.exp2(scores[frame] - new_top)
                value = kv[slot, frame, key_count : 2 * key_count, lanes]
                part = jnp.dot(
                    weight.astype(jnp.bfloat16), value, preferred_element_type=jnp.float32
                )
                added = weight if added is None else added + weight
                mixed = part if mixed is None else mixed + part
            total[head] = total[head] * alpha + added
            acc[head] = acc[head] * alpha + mixed

    own_copy.wait()
    arrivals = (
        2 + (n_head - 1) + jnp.where(z < last, 1, 0) + jnp.where(z > 0, 1, 0)
    ).astype(jnp.int32)
    pl.semaphore_wait(barrier, arrivals)
    line_sends(0, -1, "start")

    lane = lax.broadcasted_iota(jnp.int32, (tokens, key_count), 1)
    column = lax.rem(lane, VALID_COLS)
    right_half = lax.broadcasted_iota(jnp.int32, (tokens, key_count), 0) >= tokens // 2
    seen = jnp.where(right_half, column - TILE, (WINDOW * TILE - 1) - column) >= 0
    bias[...] = jnp.where(seen, 0.0, masked_value)
    top[...] = jnp.full_like(top, masked_value)
    total[...] = jnp.zeros_like(total)
    acc[...] = jnp.zeros_like(acc)

    def round_body(d, carry):
        def one(j, inner):
            real = None
            sign_up = lax.rem(j, 2)
            line_m, line_p = on_line(d - 1, -1), on_line(d - 1, 1)
            off_m, off_p = off_line(d - 2, -1), off_line(d - 2, 1)
            first = j < 2
            real = jnp.where(
                first,
                jnp.where(sign_up == 0, line_m[0].astype(jnp.int32), line_p[0].astype(jnp.int32)),
                jnp.where(sign_up == 0, off_m[0].astype(jnp.int32), off_p[0].astype(jnp.int32)),
            )
            slot = jnp.where(
                first,
                jnp.where(sign_up == 0, line_m[1], line_p[1]),
                jnp.where(sign_up == 0, off_m[1], off_p[1]),
            )

            @pl.when(real == 1)
            def _():
                attend(slot)

            return inner

        lax.fori_loop(0, 4, one, 0)
        line_sends(d, -1, "start")
        line_sends(d, 1, "start")
        cross_sends(d - 1, -1, "start")
        cross_sends(d - 1, 1, "start")
        return carry

    lax.fori_loop(1, lines + 2, round_body, 0)

    for head in range(heads):
        whole = jnp.sum(total[head], axis=1, keepdims=True)
        att[:, head * HD : (head + 1) * HD] = (acc[head] / whole).astype(jnp.bfloat16)
    weight_copy.wait()

    def product(first_row, at):
        return jnp.dot(
            att[pl.ds(pl.multiple_of(first_row, share), share), :],
            w[:, pl.ds(pl.multiple_of(at * PIECE, PIECE), PIECE)],
            preferred_element_type=jnp.float32,
        ).astype(jnp.bfloat16)

    def parcel(step, at):
        return pltpu.make_async_remote_copy(
            src_ref=outbox.at[step - 1, at],
            dst_ref=inbox.at[step - 1, at],
            send_sem=part_send.at[step - 1, at],
            recv_sem=part_recv.at[step - 1, at],
            device_id={"head": lax.rem(group + step, n_head)},
            device_id_type=MESH,
        )

    for step in range(1, n_head):

        def ship(at, carry):
            outbox[step - 1, at] = product(lax.rem(group + step, n_head) * share, at)
            parcel(step, at).start()
            return carry

        lax.fori_loop(0, pieces, ship, 0)

    def collect(at, carry):
        summed = product(group * share, at).astype(jnp.float32)
        for step in range(1, n_head):
            parcel(step, at).wait_recv()
            summed = summed + inbox[step - 1, at].astype(jnp.float32)
        out_ref[:, pl.ds(pl.multiple_of(at * PIECE, PIECE), PIECE)] = summed.astype(jnp.bfloat16)
        return carry

    lax.fori_loop(0, pieces, collect, 0)

    for step in range(1, n_head):

        def settle(at, carry):
            parcel(step, at).wait_send()
            return carry

        lax.fori_loop(0, pieces, settle, 0)

    def drain(d, carry):
        line_sends(d, -1, "wait")
        line_sends(d, 1, "wait")
        cross_sends(d, -1, "wait")
        cross_sends(d, 1, "wait")
        return carry

    lax.fori_loop(0, lines, drain, 0)


def on_device(n_height, n_head, queries, keys_values, out_weight):
    frames_dev, rows_dev, col_count, width = queries.shape
    model = out_weight.shape[1]
    heads = width // HD
    tokens = frames_dev * rows_dev * col_count
    key_count = rows_dev * VALID_COLS
    share = tokens // n_head
    pieces = model // PIECE
    assert frames_dev == 2 and rows_dev == PAD_ROWS and col_count == 4 * TILE
    assert n_height % 2 == 0 and n_height * rows_dev <= WINDOW * TILE
    side = lax.axis_index("tm")
    ordered = jnp.transpose(queries, (2, 0, 1, 3)).reshape(tokens, width)
    packed = jnp.transpose(keys_values[:, :, :, :VALID_COLS], (1, 0, 2, 3, 4))
    packed = packed.reshape(frames_dev, 2 * key_count, width)
    packed = jnp.where(side == 0, packed[::-1], packed)
    others = n_head - 1
    out = pl.pallas_call(
        functools.partial(kernel, n_height, n_head, rows_dev),
        out_shape=jax.ShapeDtypeStruct((share, model), jnp.bfloat16),
        in_specs=[
            pl.BlockSpec(memory_space=pltpu.VMEM),
            pl.BlockSpec(memory_space=pl.ANY),
            pl.BlockSpec(memory_space=pl.ANY),
        ],
        out_specs=pl.BlockSpec(memory_space=pltpu.VMEM),
        scratch_shapes=[
            pltpu.VMEM((n_height, 3, 2 * key_count, width), jnp.bfloat16),
            pltpu.VMEM((width, model), jnp.bfloat16),
            pltpu.VMEM((tokens, key_count), jnp.float32),
            pltpu.VMEM((heads, tokens, 1), jnp.float32),
            pltpu.VMEM((heads, tokens, key_count), jnp.float32),
            pltpu.VMEM((heads, tokens, HD), jnp.float32),
            pltpu.VMEM((tokens, width), jnp.bfloat16),
            pltpu.VMEM((others, pieces, share, PIECE), jnp.bfloat16),
            pltpu.VMEM((others, pieces, share, PIECE), jnp.bfloat16),
            pltpu.SemaphoreType.DMA,
            pltpu.SemaphoreType.DMA,
            pltpu.SemaphoreType.DMA((4, n_height, 2)),
            pltpu.SemaphoreType.DMA((n_height, 3)),
            pltpu.SemaphoreType.DMA((others, pieces)),
            pltpu.SemaphoreType.DMA((others, pieces)),
        ],
        compiler_params=pltpu.CompilerParams(
            collective_id=0, has_side_effects=True, vmem_limit_bytes=56 * 2**20
        ),
        name="tile_attention",
    )(ordered, packed, out_weight)
    return out.reshape(col_count // n_head, frames_dev, rows_dev, model)


def solution(mesh):
    placed = (
        P("tm", "height", None, "head"),
        P(None, "tm", "height", None, "head"),
        P("head", None),
    )
    return jax.shard_map(
        functools.partial(on_device, mesh.shape["height"], mesh.shape["head"]),
        mesh=mesh,
        in_specs=placed,
        out_specs=P("head", "tm", "height", None),
        check_vma=False,
    )
```

time: 178 us -> 94.3 us (0.53)
  waiting for transfers between devices: 127 us -> 0 us
  Pallas kernels: 0 us -> 85.1 us
  between operations: 13.7 us -> 0.03 us
  matrix products: 13.4 us -> 0 us
  other arithmetic: 8.24 us -> 0.9 us
  local copies, waits for them, and re-layouts: 13.9 us -> 6.63 us
    all_gather x1 -> x0, waiting for transfers between devices: 86.7 us -> none  [on_device(): whole_rows = lax.all_gather(keys_values, 'height', axis=2, tiled=True)]
    pallas_call x0 -> x1, Pallas kernels: none -> 85.1 us  [on_device(): pl.pallas_call(functools.partial(kernel, n_height, n_head, rows_dev), out...]
    reduce_scatter x1 -> x0, waiting for transfers between devices: 38.9 us -> none  [on_device(): lax.psum_scatter(jnp.einsum('cfrh,hd->cfrd', attended, out_weight, prefer...]
    dot_general x21 -> x0, matrix products: 13.4 us -> none  [the longest x10 4.89 us: on_device(): jnp.einsum('qd,kd->qk', head_query, head_keys, preferred_element_type=jnp...]
    concatenate x1 -> x0, other arithmetic: 5.71 us -> none  [attach_rim(): joined = jnp.concatenate([rim_frame, local_keys, rim_frame], axis=1)]
    reduce_scatter x1 -> x0, local copies, waits for them, and re-layouts: 3.72 us -> none  [on_device(): lax.psum_scatter(jnp.einsum('cfrh,hd->cfrd', attended, out_weight, prefer...]
    dynamic_slice x1 -> x0, local copies, waits for them, and re-layouts: 3.54 us -> none  [edge_frame(): return lax.dynamic_slice_in_dim(local_keys, begin, 1, 1)]
    reduce_sum x2 -> x0, other arithmetic: 2.12 us -> none  [on_device(): new_sum = jnp.sum(weights, axis=1)]
  transfers between devices with their start and end apart: 3 -> 0, of which waited for: 3 -> 0; matrix products, arithmetic and copies ran while one was open for 3% -> 0% of each run, Pallas kernels for 0% -> 0%
where the time goes in v1:
time: 94.3 us; the launch traced here: 92.7 us
  Pallas kernels  85.1 us (90%)
  local copies, waits for them, and re-layouts  6.63 us (7%)
    pallas_call x1, Pallas kernels, on_device(): pl.pallas_call(functools.partial(kernel, n_height, n_head, rows_dev), out...  85.1 us
    reshape x1, local copies, waits for them, and re-layouts, on_device(): return out.reshape(col_count // n_head, frames_dev, rows_dev, model)  3.86 us

profile of v1, /device:TPU:28, one launch (start us, length us, event | category | flops | bytes accessed | tf_op | source)
XLA Modules:
  0.0 92.7 jit_solution(16739478854332564734)
XLA Ops:
  0.0 0.0 copy-start
  0.0 1.4 %copy.6 = bf16[64,2,2,640]{3,2,1,0:T(2,128)(2,1)S(1)} copy(bf16[64,2,2,640]{3,0,2,1:T(8,128)(2,1)} %bitcast.5) | data formatting | bytes 655360 | tf_op jit(solution)/shard_map/transpose | solution.py:326
  1.4 0.9 reshape.9.q_ref
  2.2 0.0 copy-done
  2.3 0.1 slice_bitcast_fusion
  2.3 0.4 copy.7
  2.7 0.1 copy.8
  2.8 0.9 reverse_select_fusion.kv_hbm
  3.7 85.1 %tile_attention.1 = bf16[128,5120]{1,0:T(8,128)(2,1)} custom-call(bf16[256,640]{1,0:T(8,128)(2,1)} %reshape.9.q_ref, bf16[2,208,640]{2,1,0:T(8,128)(2,1)} %reverse_select_fusion.kv_hbm, bf16[640,5120]{1,0:T(8,128)(2,1)} %w_hbm.1), custom_call_target="tpu_custom_call" | custom-call | tf_op jit(solution)/shard_map/tile_attention/pallas_call | solution.py:331
  88.8 3.9 %reshape.11 = bf16[32,2,2,5120]{3,2,1,0:T(2,128)(2,1)} reshape(bf16[128,5120]{1,0:T(8,128)(2,1)} %tile_attention.1) | data formatting | bytes 2621440 | tf_op jit(solution)/shard_map/reshape | solution.py:362
Async XLA Ops:
  0.0 2.3 %copy-start = (bf16[2,2,2,64,640]{4,3,2,1,0:T(8,128)(2,1)S(1)}, bf16[2,2,2,64,640]{4,3,2,1,0:T(8,128)(2,1)}, u32[]{:S(2)}) copy-start(bf16[2,2,2,64,640]{4,3,2,1,0:T(8,128)(2,1)} %param.4) | copy-start | bytes 1966084

commit v2 on v1

--- a/solution.py
+++ b/solution.py
@@ -16,6 +16,10 @@
 MESH = pl.DeviceIdType.MESH
 UP, DOWN, ACROSS, CORE = 0, 1, 2, 3
 PIECE = 512
+ROW_CUTS = (0, 208)
+CUTS = len(ROW_CUTS) - 1
+SHARED_PIECES = 6
+SHARED_CUTS = 4
 
 masked_value = -1e30
 
@@ -43,13 +47,21 @@
     recv_sem,
     part_send,
     part_recv,
+    w_far,
+    att_far,
+    far_send,
+    pass_send,
+    far_recv,
+    att_sems,
 ):
     lines = n_height // 2
     tokens, width = q_ref.shape
     heads = width // HD
     key_count = rows_dev * VALID_COLS
     model = w.shape[1]
-    pieces = model // PIECE
+    shared = shared_width(n_head)
+    far_width = shared // SHARED_CUTS
+    pieces = (model - shared) // PIECE
     share = tokens // n_head
     last = lines - 1
 
@@ -83,7 +95,7 @@
     for step in range(1, n_head):
         greet({"head": lax.rem(group + step, n_head)})
 
-    def link(direction, slot, frame):
+    def link(direction, slot, frame, cut):
         target = {
             UP: {"height": jnp.minimum(place + 2, n_height - 1)},
             DOWN: {"height": jnp.maximum(place - 2, 0)},
@@ -91,11 +103,12 @@
             CORE: {"tm": 1 - side},
         }[direction]
         landing = 2 if direction == CORE else frame
+        span = pl.ds(ROW_CUTS[cut], ROW_CUTS[cut + 1] - ROW_CUTS[cut])
         return pltpu.make_async_remote_copy(
-            src_ref=kv.at[slot, frame],
-            dst_ref=kv.at[slot, landing],
-            send_sem=send_sem.at[direction, slot, frame],
-            recv_sem=recv_sem.at[slot, landing],
+            src_ref=kv.at[slot, frame, span],
+            dst_ref=kv.at[slot, landing, span],
+            send_sem=send_sem.at[direction, slot, frame * CUTS + cut],
+            recv_sem=recv_sem.at[slot, landing * CUTS + cut],
             device_id=target,
             device_id_type=MESH,
         )
@@ -121,61 +134,74 @@
         slot = jnp.clip(2 * zs + 1 - y, 0, n_height - 1)
         return real, slot, proxy & real
 
-    def line_sends(d, sign, act):
-        real, slot, up, down, across = on_line(d, sign)
+    def act_on(flag, copy, act):
+        @pl.when(flag)
+        def _():
+            getattr(copy, act)()
+
+    def line_sends(d, act):
+        sides = [on_line(d, -1), on_line(d, 1)]
+        _, proxy_slot, proxy = off_line(0, -1)
         for frame in (0, 1):
-            if act == "start":
-
-                @pl.when(real & (d > 0))
-                def _():
-                    link(UP, slot, frame).wait_recv()
-
-            for flag, direction in ((up, UP), (down, DOWN), (across, ACROSS)):
-
-                @pl.when(flag)
-                def _():
-                    copy = link(direction, slot, frame)
-                    copy.start() if act == "start" else copy.wait_send()
-
-            if frame == 0:
-
-                @pl.when(real)
-                def _():
-                    copy = link(CORE, slot, 0)
-                    copy.start() if act == "start" else copy.wait_send()
-
-    def cross_sends(d, sign, act):
-        real, slot, proxy = off_line(d, sign)
+            for cut in range(CUTS):
+                for real, slot, up, down, across in sides:
+                    if act == "start":
+                        act_on(real & (d > 0), link(UP, slot, frame, cut), "wait_recv")
+                    act_on(up, link(UP, slot, frame, cut), act)
+                    act_on(down, link(DOWN, slot, frame, cut), act)
+                    act_on(across, link(ACROSS, slot, frame, cut), act)
+                    if frame == 0:
+                        act_on(real, link(CORE, slot, 0, cut), act)
+                now = proxy & (d == 1)
+                if act == "start":
+                    act_on(now, link(ACROSS, proxy_slot, frame, cut), "wait_recv")
+                act_on(now, link(DOWN, proxy_slot, frame, cut), act)
+                if frame == 0:
+                    act_on(now, link(CORE, proxy_slot, 0, cut), act)
+
+    def cross_sends(d, act):
+        sides = [off_line(d, -1), off_line(d, 1)]
         for frame in (0, 1):
-            if act == "start":
-
-                @pl.when(real)
-                def _():
-                    link(ACROSS, slot, frame).wait_recv()
-
-            @pl.when(proxy)
-            def _():
-                copy = link(DOWN, slot, frame)
-                copy.start() if act == "start" else copy.wait_send()
-
-            if frame == 0:
-
-                @pl.when(real)
-                def _():
-                    copy = link(CORE, slot, 0)
-                    copy.start() if act == "start" else copy.wait_send()
-
-    factor = math.log2(math.e) / math.sqrt(HD)
-
-    def attend(slot):
-        pltpu.make_async_remote_copy(
-            src_ref=kv.at[slot, 2],
-            dst_ref=kv.at[slot, 2],
-            send_sem=send_sem.at[CORE, slot, 0],
-            recv_sem=recv_sem.at[slot, 2],
+            for cut in range(CUTS):
+                for real, slot, proxy in sides:
+                    plain = real & jnp.logical_not(proxy)
+                    if act == "start":
+                        act_on(plain, link(ACROSS, slot, frame, cut), "wait_recv")
+                    if frame == 0:
+                        act_on(plain, link(CORE, slot, 0, cut), act)
+
+    def far_weight(step):
+        at = 2 * side + step
+        first = pl.multiple_of(model - shared + at * far_width, HD)
+        return pltpu.make_async_remote_copy(
+            src_ref=w_hbm.at[:, pl.ds(first, far_width)],
+            dst_ref=w_far.at[at],
+            send_sem=far_send.at[step],
+            recv_sem=far_recv.at[at],
+            device_id={"head": 1 - group},
+            device_id_type=MESH,
+        )
+
+    def pass_weight(step, owner):
+        at = 2 * owner + step
+        return pltpu.make_async_remote_copy(
+            src_ref=w_far.at[at],
+            dst_ref=w_far.at[at],
+            send_sem=pass_send.at[step],
+            recv_sem=far_recv.at[at],
             device_id={"tm": 1 - side},
             device_id_type=MESH,
-        ).wait_recv()
+        )
+
+    def relay_weight(step):
+        far_weight(step).wait_recv()
+        pass_weight(step, side).start()
+
+    factor = math.log2(math.e) / math.sqrt(HD)
+
+    def attend(slot):
+        for cut in range(CUTS):
+            link(CORE, slot, 0, cut).wait_recv()
         for head in range(heads):
             lanes = slice(head * HD, (head + 1) * HD)
             query = q_ref[:, lanes]
@@ -209,7 +235,10 @@
         2 + (n_head - 1) + jnp.where(z < last, 1, 0) + jnp.where(z > 0, 1, 0)
     ).astype(jnp.int32)
     pl.semaphore_wait(barrier, arrivals)
-    line_sends(0, -1, "start")
+    line_sends(0, "start")
+    if shared:
+        far_weight(0).start()
+        far_weight(1).start()
 
     lane = lax.broadcasted_iota(jnp.int32, (tokens, key_count), 1)
     column = lax.rem(lane, VALID_COLS)
@@ -221,6 +250,16 @@
     acc[...] = jnp.zeros_like(acc)
 
     def round_body(d, carry):
+        if shared:
+
+            @pl.when(d == 3)
+            def _():
+                relay_weight(0)
+
+            @pl.when(d == lines + 1)
+            def _():
+                relay_weight(1)
+
         def one(j, inner):
             real = None
             sign_up = lax.rem(j, 2)
@@ -245,10 +284,8 @@
             return inner
 
         lax.fori_loop(0, 4, one, 0)
-        line_sends(d, -1, "start")
-        line_sends(d, 1, "start")
-        cross_sends(d - 1, -1, "start")
-        cross_sends(d - 1, 1, "start")
+        line_sends(d, "start")
+        cross_sends(d - 1, "start")
         return carry
 
     lax.fori_loop(1, lines + 2, round_body, 0)
@@ -275,6 +312,18 @@
             device_id_type=MESH,
         )
 
+    if shared:
+        far_rows = pl.ds(pl.multiple_of((1 - group) * share, share), share)
+        att_copy = pltpu.make_async_remote_copy(
+            src_ref=att.at[far_rows],
+            dst_ref=att_far,
+            send_sem=att_sems.at[0],
+            recv_sem=att_sems.at[1],
+            device_id={"head": 1 - group},
+            device_id_type=MESH,
+        )
+        att_copy.start()
+
     for step in range(1, n_head):
 
         def ship(at, carry):
@@ -283,6 +332,20 @@
             return carry
 
         lax.fori_loop(0, pieces, ship, 0)
+
+    if shared:
+        own_rows = pl.ds(pl.multiple_of(group * share, share), share)
+        pass_weight(0, 1 - side).wait_recv()
+        pass_weight(1, 1 - side).wait_recv()
+        att_copy.wait_recv()
+        for at in range(SHARED_CUTS):
+            first = model - shared + at * far_width
+            span = slice(first, first + far_width)
+            near = jnp.dot(att[own_rows, :], w[:, span], preferred_element_type=jnp.float32)
+            far = jnp.dot(att_far[...], w_far[at], preferred_element_type=jnp.float32)
+            near = near.astype(jnp.bfloat16).astype(jnp.float32)
+            far = far.astype(jnp.bfloat16).astype(jnp.float32)
+            out_ref[:, span] = (near + far).astype(jnp.bfloat16)
 
     def collect(at, carry):
         summed = product(group * share, at).astype(jnp.float32)
@@ -302,14 +365,22 @@
 
         lax.fori_loop(0, pieces, settle, 0)
 
+    if shared:
+        att_copy.wait_send()
+        for step in range(2):
+            far_weight(step).wait_send()
+            pass_weight(step, side).wait_send()
+
     def drain(d, carry):
-        line_sends(d, -1, "wait")
-        line_sends(d, 1, "wait")
-        cross_sends(d, -1, "wait")
-        cross_sends(d, 1, "wait")
+        line_sends(d, "wait_send")
+        cross_sends(d, "wait_send")
         return carry
 
     lax.fori_loop(0, lines, drain, 0)
+
+
+def shared_width(n_head):
+    return SHARED_PIECES * PIECE if n_head == 2 else 0
 
 
 def on_device(n_height, n_head, queries, keys_values, out_weight):
@@ -319,7 +390,9 @@
     tokens = frames_dev * rows_dev * col_count
     key_count = rows_dev * VALID_COLS
     share = tokens // n_head
-    pieces = model // PIECE
+    shared = shared_width(n_head)
+    far_width = shared // SHARED_CUTS
+    pieces = (model - shared) // PIECE
     assert frames_dev == 2 and rows_dev == PAD_ROWS and col_count == 4 * TILE
     assert n_height % 2 == 0 and n_height * rows_dev <= WINDOW * TILE
     side = lax.axis_index("tm")
@@ -349,10 +422,16 @@
             pltpu.VMEM((others, pieces, share, PIECE), jnp.bfloat16),
             pltpu.SemaphoreType.DMA,
             pltpu.SemaphoreType.DMA,
-            pltpu.SemaphoreType.DMA((4, n_height, 2)),
-            pltpu.SemaphoreType.DMA((n_height, 3)),
+            pltpu.SemaphoreType.DMA((4, n_height, 2 * CUTS)),
+            pltpu.SemaphoreType.DMA((n_height, 3 * CUTS)),
             pltpu.SemaphoreType.DMA((others, pieces)),
             pltpu.SemaphoreType.DMA((others, pieces)),
+            pltpu.VMEM((SHARED_CUTS, width, max(far_width, HD)), jnp.bfloat16),
+            pltpu.VMEM((share, width), jnp.bfloat16),
+            pltpu.SemaphoreType.DMA((2,)),
+            pltpu.SemaphoreType.DMA((2,)),
+            pltpu.SemaphoreType.DMA((SHARED_CUTS,)),
+            pltpu.SemaphoreType.DMA((2,)),
         ],
         compiler_params=pltpu.CompilerParams(
             collective_id=0, has_side_effects=True, vmem_limit_bytes=56 * 2**20

time: 94.3 us -> 79.3 us (0.84); the launches traced: 92.7 us -> 79 us
  Pallas kernels: 85.1 us -> 71.5 us
    pallas_call x1, Pallas kernels: 85.1 us -> 71.5 us  [on_device(): pl.pallas_call(functools.partial(kernel, n_height, n_head, rows_dev), out...]
where the time goes in v2:
time: 79.3 us; the launch traced here: 79 us
  Pallas kernels  71.5 us (90%)
  local copies, waits for them, and re-layouts  6.63 us (8%)
  other arithmetic  0.9 us (1%)
    pallas_call x1, Pallas kernels, on_device(): pl.pallas_call(functools.partial(kernel, n_height, n_head, rows_dev), out...  71.5 us
    reshape x1, local copies, waits for them, and re-layouts, on_device(): return out.reshape(col_count // n_head, frames_dev, rows_dev, model)  3.86 us

profile of v2, /device:TPU:28, one launch (start us, length us, event | category | flops | bytes accessed | tf_op | source)
XLA Modules:
  0.0 79.0 jit_solution(4691334989264766215)
XLA Ops:
  0.0 0.0 copy-start
  0.0 1.4 %copy.6 = bf16[64,2,2,640]{3,2,1,0:T(2,128)(2,1)S(1)} copy(bf16[64,2,2,640]{3,0,2,1:T(8,128)(2,1)} %bitcast.5) | data formatting | bytes 655360 | tf_op jit(solution)/shard_map/transpose | solution.py:399
  1.4 0.9 %reshape.9.q_ref = bf16[256,640]{1,0:T(8,128)(2,1)} reshape(bf16[64,2,2,640]{3,2,1,0:T(2,128)(2,1)S(1)} %copy.6) | data formatting | bytes 655360 | tf_op jit(solution)/shard_map/reshape | solution.py:399
  2.2 0.0 copy-done
  2.3 0.1 slice_bitcast_fusion
  2.3 0.4 copy.7
  2.7 0.1 copy.8
  2.8 0.9 %reverse_select_fusion.kv_hbm = bf16[2,208,640]{2,1,0:T(8,128)(2,1)} fusion(bf16[2,208,640]{2,1,0:T(8,128)(2,1)S(1)} %copy.8, pred[]{:T(512)S(6)} %eq.3), kind=kLoop, calls=%fused_computation | loop fusion | flops 266240 | bytes 1064961 | tf_op jit(solution)/shard_map/jit(_where)/select_n | solution.py:402
  3.7 71.5 %tile_attention.1 = bf16[128,5120]{1,0:T(8,128)(2,1)} custom-call(bf16[256,640]{1,0:T(8,128)(2,1)} %reshape.9.q_ref, bf16[2,208,640]{2,1,0:T(8,128)(2,1)} %reverse_select_fusion.kv_hbm, bf16[640,5120]{1,0:T(8,128)(2,1)} %w_hbm.1), custom_call_target="tpu_custom_call" | custom-call | tf_op jit(solution)/shard_map/tile_attention/pallas_call | solution.py:404
  75.2 3.9 %reshape.11 = bf16[32,2,2,5120]{3,2,1,0:T(2,128)(2,1)} reshape(bf16[128,5120]{1,0:T(8,128)(2,1)} %tile_attention.1) | data formatting | bytes 2621440 | tf_op jit(solution)/shard_map/reshape | solution.py:441
Async XLA Ops:
  0.0 2.3 %copy-start = (bf16[2,2,2,64,640]{4,3,2,1,0:T(8,128)(2,1)S(1)}, bf16[2,2,2,64,640]{4,3,2,1,0:T(8,128)(2,1)}, u32[]{:S(2)}) copy-start(bf16[2,2,2,64,640]{4,3,2,1,0:T(8,128)(2,1)} %param.4) | copy-start | bytes 1966084

commit v3 on v2

--- a/solution.py
+++ b/solution.py
@@ -20,6 +20,7 @@
 CUTS = len(ROW_CUTS) - 1
 SHARED_PIECES = 6
 SHARED_CUTS = 4
+COPY_CUTS = 4
 
 masked_value = -1e30
 
@@ -28,7 +29,7 @@
     n_height,
     n_head,
     rows_dev,
-    q_ref,
+    raw_ref,
     kv_hbm,
     w_hbm,
     out_ref,
@@ -53,9 +54,11 @@
     pass_send,
     far_recv,
     att_sems,
+    q_ref,
+    own_raw,
 ):
     lines = n_height // 2
-    tokens, width = q_ref.shape
+    tokens, width = raw_ref.shape
     heads = width // HD
     key_count = rows_dev * VALID_COLS
     model = w.shape[1]
@@ -74,7 +77,7 @@
 
     weight_copy = pltpu.make_async_copy(w_hbm, w, w_sem)
     weight_copy.start()
-    own_copy = pltpu.make_async_copy(kv_hbm, kv.at[place, 0:2], own_sem)
+    own_copy = pltpu.make_async_copy(kv_hbm, own_raw, own_sem)
     own_copy.start()
 
     barrier = pltpu.get_barrier_semaphore()
@@ -231,6 +234,13 @@
             acc[head] = acc[head] * alpha + mixed
 
     own_copy.wait()
+    for frame, held in ((0, 1 - side), (1, side)):
+        for kind in range(2):
+            for row in range(rows_dev):
+                first = (kind * rows_dev + row) * VALID_COLS
+                kv[place, frame, first : first + VALID_COLS, :] = own_raw[
+                    kind, held, row, 0:VALID_COLS, :
+                ]
     arrivals = (
         2 + (n_head - 1) + jnp.where(z < last, 1, 0) + jnp.where(z > 0, 1, 0)
     ).astype(jnp.int32)
@@ -239,6 +249,15 @@
     if shared:
         far_weight(0).start()
         far_weight(1).start()
+
+    runs = 2 * rows_dev
+    source = lax.broadcasted_iota(jnp.int32, (tokens, tokens), 1)
+    wanted = lax.broadcasted_iota(jnp.int32, (tokens, tokens), 0)
+    wanted = lax.rem(wanted, runs) * (tokens // runs) + lax.div(wanted, runs)
+    moved = jnp.where(source == wanted, 1.0, 0.0).astype(jnp.bfloat16)
+    q_ref[...] = jnp.dot(
+        moved, raw_ref[...], preferred_element_type=jnp.float32
+    ).astype(jnp.bfloat16)
 
     lane = lax.broadcasted_iota(jnp.int32, (tokens, key_count), 1)
     column = lax.rem(lane, VALID_COLS)
@@ -295,6 +314,9 @@
         att[:, head * HD : (head + 1) * HD] = (acc[head] / whole).astype(jnp.bfloat16)
     weight_copy.wait()
 
+    def paired(value):
+        return value.reshape(share // rows_dev, rows_dev, value.shape[1]).astype(jnp.bfloat16)
+
     def product(first_row, at):
         return jnp.dot(
             att[pl.ds(pl.multiple_of(first_row, share), share), :],
@@ -345,14 +367,14 @@
             far = jnp.dot(att_far[...], w_far[at], preferred_element_type=jnp.float32)
             near = near.astype(jnp.bfloat16).astype(jnp.float32)
             far = far.astype(jnp.bfloat16).astype(jnp.float32)
-            out_ref[:, span] = (near + far).astype(jnp.bfloat16)
+            out_ref[:, :, span] = paired(near + far)
 
     def collect(at, carry):
         summed = product(group * share, at).astype(jnp.float32)
         for step in range(1, n_head):
             parcel(step, at).wait_recv()
             summed = summed + inbox[step - 1, at].astype(jnp.float32)
-        out_ref[:, pl.ds(pl.multiple_of(at * PIECE, PIECE), PIECE)] = summed.astype(jnp.bfloat16)
+        out_ref[:, :, pl.ds(pl.multiple_of(at * PIECE, PIECE), PIECE)] = paired(summed)
         return carry
 
     lax.fori_loop(0, pieces, collect, 0)
@@ -377,6 +399,21 @@
         return carry
 
     lax.fori_loop(0, lines, drain, 0)
+
+
+def copy_kernel(in_ref, out_ref, held, sems):
+    rows = in_ref.shape[0] // COPY_CUTS
+    spans = [pl.ds(cut * rows, rows) for cut in range(COPY_CUTS)]
+    loads, stores = [], []
+    for cut, span in enumerate(spans):
+        loads.append(pltpu.make_async_copy(in_ref.at[span], held.at[span], sems.at[0, cut]))
+        stores.append(pltpu.make_async_copy(held.at[span], out_ref.at[span], sems.at[1, cut]))
+        loads[cut].start()
+    for load, store in zip(loads, stores):
+        load.wait()
+        store.start()
+    for store in stores:
+        store.wait()
 
 
 def shared_width(n_head):
@@ -395,15 +432,11 @@
     pieces = (model - shared) // PIECE
     assert frames_dev == 2 and rows_dev == PAD_ROWS and col_count == 4 * TILE
     assert n_height % 2 == 0 and n_height * rows_dev <= WINDOW * TILE
-    side = lax.axis_index("tm")
-    ordered = jnp.transpose(queries, (2, 0, 1, 3)).reshape(tokens, width)
-    packed = jnp.transpose(keys_values[:, :, :, :VALID_COLS], (1, 0, 2, 3, 4))
-    packed = packed.reshape(frames_dev, 2 * key_count, width)
-    packed = jnp.where(side == 0, packed[::-1], packed)
+    raw = queries.reshape(tokens, width)
     others = n_head - 1
     out = pl.pallas_call(
         functools.partial(kernel, n_height, n_head, rows_dev),
-        out_shape=jax.ShapeDtypeStruct((share, model), jnp.bfloat16),
+        out_shape=jax.ShapeDtypeStruct((share // rows_dev, rows_dev, model), jnp.bfloat16),
         in_specs=[
             pl.BlockSpec(memory_space=pltpu.VMEM),
             pl.BlockSpec(memory_space=pl.ANY),
@@ -432,12 +465,25 @@
             pltpu.SemaphoreType.DMA((2,)),
             pltpu.SemaphoreType.DMA((SHARED_CUTS,)),
             pltpu.SemaphoreType.DMA((2,)),
+            pltpu.VMEM((tokens, width), jnp.bfloat16),
+            pltpu.VMEM(keys_values.shape, jnp.bfloat16),
         ],
         compiler_params=pltpu.CompilerParams(
             collective_id=0, has_side_effects=True, vmem_limit_bytes=56 * 2**20
         ),
         name="tile_attention",
-    )(ordered, packed, out_weight)
+    )(raw, keys_values, out_weight)
+    out = pl.pallas_call(
+        copy_kernel,
+        out_shape=jax.ShapeDtypeStruct(out.shape, out.dtype),
+        in_specs=[pl.BlockSpec(memory_space=pl.ANY)],
+        out_specs=pl.BlockSpec(memory_space=pl.ANY),
+        scratch_shapes=[
+            pltpu.VMEM(out.shape, out.dtype),
+            pltpu.SemaphoreType.DMA((2, COPY_CUTS)),
+        ],
+        name="hand_over",
+    )(out)
     return out.reshape(col_count // n_head, frames_dev, rows_dev, model)
 
 

time: 79.3 us -> 73.9 us (0.932)
  local copies, waits for them, and re-layouts: 6.63 us -> 0 us
  Pallas kernels: 71.5 us -> 73.7 us
  other arithmetic: 0.9 us -> 0 us
    reshape x3 -> x0, local copies, waits for them, and re-layouts: 4.79 us -> none  [the longest x1 3.86 us: on_device(): return out.reshape(col_count // n_head, frames_dev, rows_dev, model)]
    pallas_call x0 -> x1, Pallas kernels: none -> 2.09 us  [on_device(): pl.pallas_call(copy_kernel, out_shape=jax.ShapeDtypeStruct(out.shape, out...]
    transpose x3 -> x0, local copies, waits for them, and re-layouts: 1.84 us -> none  [the longest x1 1.38 us: on_device(): ordered = jnp.transpose(queries, (2, 0, 1, 3)).reshape(tokens, width)]
    select_n x1 -> x0, other arithmetic: 0.9 us -> none  [on_device(): packed = jnp.where(side == 0, packed[::-1], packed)]
where the time goes in v3:
time: 73.9 us; the launch traced here: 73.7 us
  Pallas kernels  73.7 us (100%)
    pallas_call x1, Pallas kernels, on_device(): pl.pallas_call(functools.partial(kernel, n_height, n_head, rows_dev), out...  71.7 us
    pallas_call x1, Pallas kernels, on_device(): pl.pallas_call(copy_kernel, out_shape=jax.ShapeDtypeStruct(out.shape, out...  2.09 us

profile of v3, /device:TPU:28, one launch (start us, length us, event | category | flops | bytes accessed | tf_op | source)
XLA Modules:
  0.0 73.7 jit_solution(4625726227226265249)
XLA Ops:
  0.0 71.7 %tile_attention.1.in_ref = bf16[64,2,5120]{2,1,0:T(2,128)(2,1)} custom-call(bf16[256,640]{1,0:T(8,128)(2,1)} %bitcast.2, bf16[2,2,2,64,640]{4,3,2,1,0:T(8,128)(2,1)} %kv_hbm.1, bf16[640,5120]{1,0:T(8,128)(2,1)} %w_hbm.1), custom_call_target="tpu_custom_call" | custom-call | tf_op jit(solution)/shard_map/tile_attention/pallas_call | solution.py:437
  71.7 2.1 %hand_over.1 = bf16[64,2,5120]{2,1,0:T(2,128)(2,1)} custom-call(bf16[64,2,5120]{2,1,0:T(2,128)(2,1)} %tile_attention.1.in_ref), custom_call_target="tpu_custom_call" | custom-call | tf_op jit(solution)/shard_map/hand_over/pallas_call | solution.py:476

commit v4 on v3

--- a/solution.py
+++ b/solution.py
@@ -126,7 +126,8 @@
         up = real & (z < last) & ((sign < 0) | (d == 0))
         down = real & (z > 0) & ((sign > 0) | (d == 0))
         across = real & ((zs != last) | ((z == last) & (y == 0)))
-        return real, slot, up, down, across
+        whole = across & ((zs != 0) | (z == 0) | (y == 1))
+        return real, slot, up, down, (across, whole)
 
     def off_line(d, sign):
         zs = z + sign * d
@@ -135,7 +136,8 @@
         if sign > 0:
             real = real & (d > 0)
         slot = jnp.clip(2 * zs + 1 - y, 0, n_height - 1)
-        return real, slot, proxy & real
+        climbs = real & (zs == 0) & (y == 1) & (z < last)
+        return real, slot, proxy & real, climbs
 
     def act_on(flag, copy, act):
         @pl.when(flag)
@@ -144,7 +146,7 @@
 
     def line_sends(d, act):
         sides = [on_line(d, -1), on_line(d, 1)]
-        _, proxy_slot, proxy = off_line(0, -1)
+        _, proxy_slot, proxy, _ = off_line(0, -1)
         for frame in (0, 1):
             for cut in range(CUTS):
                 for real, slot, up, down, across in sides:
@@ -152,7 +154,7 @@
                         act_on(real & (d > 0), link(UP, slot, frame, cut), "wait_recv")
                     act_on(up, link(UP, slot, frame, cut), act)
                     act_on(down, link(DOWN, slot, frame, cut), act)
-                    act_on(across, link(ACROSS, slot, frame, cut), act)
+                    act_on(across[frame], link(ACROSS, slot, frame, cut), act)
                     if frame == 0:
                         act_on(real, link(CORE, slot, 0, cut), act)
                 now = proxy & (d == 1)
@@ -166,10 +168,12 @@
         sides = [off_line(d, -1), off_line(d, 1)]
         for frame in (0, 1):
             for cut in range(CUTS):
-                for real, slot, proxy in sides:
+                for real, slot, proxy, climbs in sides:
                     plain = real & jnp.logical_not(proxy)
                     if act == "start":
                         act_on(plain, link(ACROSS, slot, frame, cut), "wait_recv")
+                    if frame == 1:
+                        act_on(climbs, link(UP, slot, frame, cut), act)
                     if frame == 0:
                         act_on(plain, link(CORE, slot, 0, cut), act)
 

time: 73.9 us -> 70.8 us (0.958)
  Pallas kernels: 73.7 us -> 70.6 us
    pallas_call x1, Pallas kernels: 71.7 us -> 68.5 us  [on_device(): pl.pallas_call(functools.partial(kernel, n_height, n_head, rows_dev), out...]
where the time goes in v4:
time: 70.8 us; the launch traced here: 70.6 us
  Pallas kernels  70.6 us (100%)
    pallas_call x1, Pallas kernels, on_device(): pl.pallas_call(functools.partial(kernel, n_height, n_head, rows_dev), out...  68.5 us
    pallas_call x1, Pallas kernels, on_device(): pl.pallas_call(copy_kernel, out_shape=jax.ShapeDtypeStruct(out.shape, out...  2.09 us

profile of v4, /device:TPU:28, one launch (start us, length us, event | category | flops | bytes accessed | tf_op | source)
XLA Modules:
  0.0 70.6 jit_solution(2541709956676688910)
XLA Ops:
  0.0 68.5 %tile_attention.1.in_ref = bf16[64,2,5120]{2,1,0:T(2,128)(2,1)} custom-call(bf16[256,640]{1,0:T(8,128)(2,1)} %bitcast.2, bf16[2,2,2,64,640]{4,3,2,1,0:T(8,128)(2,1)} %kv_hbm.1, bf16[640,5120]{1,0:T(8,128)(2,1)} %w_hbm.1), custom_call_target="tpu_custom_call" | custom-call | tf_op jit(solution)/shard_map/tile_attention/pallas_call | solution.py:441
  68.5 2.1 %hand_over.1 = bf16[64,2,5120]{2,1,0:T(2,128)(2,1)} custom-call(bf16[64,2,5120]{2,1,0:T(2,128)(2,1)} %tile_attention.1.in_ref), custom_call_target="tpu_custom_call" | custom-call | tf_op jit(solution)/shard_map/hand_over/pallas_call | solution.py:480

commit v5 on v4

--- a/solution.py
+++ b/solution.py
@@ -20,7 +20,6 @@
 CUTS = len(ROW_CUTS) - 1
 SHARED_PIECES = 6
 SHARED_CUTS = 4
-COPY_CUTS = 4
 
 masked_value = -1e30
 
@@ -405,21 +404,6 @@
     lax.fori_loop(0, lines, drain, 0)
 
 
-def copy_kernel(in_ref, out_ref, held, sems):
-    rows = in_ref.shape[0] // COPY_CUTS
-    spans = [pl.ds(cut * rows, rows) for cut in range(COPY_CUTS)]
-    loads, stores = [], []
-    for cut, span in enumerate(spans):
-        loads.append(pltpu.make_async_copy(in_ref.at[span], held.at[span], sems.at[0, cut]))
-        stores.append(pltpu.make_async_copy(held.at[span], out_ref.at[span], sems.at[1, cut]))
-        loads[cut].start()
-    for load, store in zip(loads, stores):
-        load.wait()
-        store.start()
-    for store in stores:
-        store.wait()
-
-
 def shared_width(n_head):
     return SHARED_PIECES * PIECE if n_head == 2 else 0
 
@@ -440,7 +424,7 @@
     others = n_head - 1
     out = pl.pallas_call(
         functools.partial(kernel, n_height, n_head, rows_dev),
-        out_shape=jax.ShapeDtypeStruct((share // rows_dev, rows_dev, model), jnp.bfloat16),
+        out_shape=pltpu.VMEM((share // rows_dev, rows_dev, model), jnp.bfloat16),
         in_specs=[
             pl.BlockSpec(memory_space=pltpu.VMEM),
             pl.BlockSpec(memory_space=pl.ANY),
@@ -477,17 +461,6 @@
         ),
         name="tile_attention",
     )(raw, keys_values, out_weight)
-    out = pl.pallas_call(
-        copy_kernel,
-        out_shape=jax.ShapeDtypeStruct(out.shape, out.dtype),
-        in_specs=[pl.BlockSpec(memory_space=pl.ANY)],
-        out_specs=pl.BlockSpec(memory_space=pl.ANY),
-        scratch_shapes=[
-            pltpu.VMEM(out.shape, out.dtype),
-            pltpu.SemaphoreType.DMA((2, COPY_CUTS)),
-        ],
-        name="hand_over",
-    )(out)
     return out.reshape(col_count // n_head, frames_dev, rows_dev, model)
 
 

time: 70.8 us -> 68.7 us (0.970)
  Pallas kernels: 70.6 us -> 67.4 us
  local copies, waits for them, and re-layouts: 0 us -> 1.06 us
    pallas_call x1 -> x0, Pallas kernels: 2.09 us -> none  [on_device(): pl.pallas_call(copy_kernel, out_shape=jax.ShapeDtypeStruct(out.shape, out...]
    pallas_call x1, Pallas kernels: 68.5 us -> 67.4 us  [on_device(): pl.pallas_call(functools.partial(kernel, n_height, n_head, rows_dev), out...]
    unnamed x0 -> x1, local copies, waits for them, and re-layouts: none -> 1.06 us
where the time goes in v5:
time: 68.7 us; the launch traced here: 68.5 us
  Pallas kernels  67.4 us (98%)
  local copies, waits for them, and re-layouts  1.06 us (2%)
    pallas_call x1, Pallas kernels, on_device(): pl.pallas_call(functools.partial(kernel, n_height, n_head, rows_dev), out...  67.4 us

profile of v5, /device:TPU:28, one launch (start us, length us, event | category | flops | bytes accessed | tf_op | source)
XLA Modules:
  0.0 68.5 jit_solution(4198050300842837856)
XLA Ops:
  0.0 67.4 %tile_attention.1 = bf16[64,2,5120]{2,1,0:T(2,128)(2,1)S(1)} custom-call(bf16[256,640]{1,0:T(8,128)(2,1)} %bitcast.3, bf16[2,2,2,64,640]{4,3,2,1,0:T(8,128)(2,1)} %kv_hbm.1, bf16[640,5120]{1,0:T(8,128)(2,1)} %w_hbm.1), custom_call_target="tpu_custom_call" | custom-call | tf_op jit(solution)/shard_map/tile_attention/pallas_call | solution.py:425
  67.4 1.1 %copy.5 = bf16[32,2,2,5120]{3,2,1,0:T(2,128)(2,1)} copy(bf16[32,2,2,5120]{3,2,1,0:T(2,128)(2,1)S(1)} %bitcast.2) | data formatting | bytes 2621440
